TPU v7x, 128 devices: a whole 4x4x4 slice. The times are simulated.
128 devices in a mesh: freq: 8 (over y, z_lo), rows: 16 (over z_hi, x, core).
Axes of the slice: x: 4, y: 4, z: 4 (z_hi: 2, z_lo: 2; z = z_hi * 2 + z_lo), core: 2. Of those that a mesh axis runs over, the one named last changes fastest.
Arguments:
- refl: bfloat16 [2, 16, 4608, 4608], P(None, 'freq', 'rows'), may hold values from -0.125 to 0.125
- refl_scale: float32 [16, 4608, 36], P('freq', 'rows'), may hold values from 0.5 to 4
- focus: bfloat16 [16, 4608, 128], P('freq', 'rows'), may hold values from -6 to 6
- first_mute: int32 [4608, 64], P('rows'), may hold values from 128 to 1023
- second_mute: int32 [64, 4608], P('freq', 'rows'), may hold values from 256 to 1023
Outputs:
- focus_next: float32 [64, 4608, 1024], P('freq', 'rows')
All inputs are finite; a program needn't handle non-finite values.
Results may differ from a plain program's by a relative error of at most 0.0085.
Values may be sent and summed in bfloat16 or wider, within the bound.
No kernel may reach another device: no remote copies, remote signals or barrier semaphores. Data moves between devices by JAX's collectives and lax.ppermute only.
A program may use at most 128 MiB of HBM per device.

v0:
```python
import math
import jax
import jax.numpy as jnp
from jax import lax
from jax.sharding import PartitionSpec as P

NT = 1024
LOWBIN = 24


def tables(freq_total):
    time_index = jnp.arange(NT, dtype=jnp.int32)
    freq_bins = LOWBIN + jnp.arange(freq_total, dtype=jnp.int32)
    phases = (freq_bins[:, None] * time_index[None, :] % NT).astype(jnp.float32) * (
        2.0 * math.pi / NT
    )
    inward = 1.0 / math.sqrt(2.0 * freq_total)
    outward = 2.0 / (NT * inward)
    basis_rows = jnp.concatenate([jnp.cos(phases), -jnp.sin(phases)], 0)
    return (basis_rows.T * inward, basis_rows * outward)


def split_basis(basis):
    upper = basis.astype(jnp.bfloat16)
    lower = (basis - upper.astype(jnp.float32)).astype(jnp.bfloat16)
    return (upper, lower)


def decode(quantized, block_scale):
    blocks = block_scale.shape[-1]
    reshaped = quantized.reshape(quantized.shape[:3] + (blocks, quantized.shape[3] // blocks))
    return (
        (reshaped * block_scale[None, :, :, :, None]).astype(jnp.bfloat16).reshape(quantized.shape)
    )


def combine_first(direct, crossed, points):
    return jnp.concatenate(
        [
            direct[..., :points] - crossed[..., points:],
            direct[..., points:] + crossed[..., :points],
        ],
        -1,
    )


def combine_second(direct, crossed, points):
    return jnp.concatenate(
        [
            direct[..., :points] + crossed[..., points:],
            direct[..., points:] - crossed[..., :points],
        ],
        -1,
    )


def mute_pass(samples, cutoff, inverse, forward):
    upper, lower = split_basis(inverse)
    traces = jnp.dot(upper, samples, preferred_element_type=jnp.float32) + jnp.dot(
        lower, samples, preferred_element_type=jnp.float32
    )
    time_index = jnp.arange(NT, dtype=jnp.int32)
    kept = jnp.where(time_index[:, None] < cutoff[None, :], traces, 0.0)
    return jnp.dot(forward, kept, precision=lax.Precision.HIGHEST).astype(jnp.bfloat16)


def on_device(refl, refl_scale, focus, first_mute, second_mute):
    groups = lax.axis_size("freq")
    freq_dev = refl.shape[1]
    rows_dev = refl.shape[2]
    points = focus.shape[2] // 2
    freq_total = freq_dev * groups
    inverse, forward = tables(freq_total)
    decoded = decode(refl, refl_scale)
    columns = decoded
    paired = jnp.einsum(
        "kfsn,fnc->kfsc",
        columns,
        lax.all_gather(focus, "rows", axis=1, tiled=True),
        preferred_element_type=jnp.float32,
    )
    focused = combine_first(paired[0], paired[1], points).astype(jnp.bfloat16)
    self_index = lax.axis_index("freq")
    block_size = points // groups
    exchanged = lax.all_to_all(
        focused.reshape(freq_dev, rows_dev, 2, points),
        "freq",
        split_axis=3,
        concat_axis=0,
        tiled=True,
    )
    samples = exchanged.transpose(2, 0, 1, 3).reshape(2 * freq_total, rows_dev * block_size)
    cutoff = lax.dynamic_slice_in_dim(first_mute, self_index * block_size, block_size, 1).reshape(
        rows_dev * block_size
    )
    spectra = mute_pass(samples, cutoff, inverse, forward)
    spectra = spectra.reshape(2, freq_total, rows_dev, block_size).transpose(1, 2, 0, 3)
    returned = lax.all_to_all(spectra, "freq", split_axis=0, concat_axis=3, tiled=True).reshape(
        freq_dev, rows_dev, 2 * points
    )
    point_share = points // groups
    columns = decoded
    products = jnp.einsum("kfsn,fsc->knfc", columns, returned, preferred_element_type=jnp.float32)
    summed = lax.psum_scatter(
        combine_second(products[0], products[1], points), "rows", scatter_dimension=0, tiled=True
    )
    adjoint_half = summed.astype(jnp.bfloat16).reshape(rows_dev, freq_dev, 2, points)
    regrouped = lax.all_to_all(adjoint_half, "freq", split_axis=3, concat_axis=1, tiled=True)
    final_samples = regrouped.transpose(3, 0, 2, 1).reshape(point_share * rows_dev, 2 * freq_total)
    upper, lower = split_basis(inverse.T)
    traces = jnp.dot(final_samples, upper, preferred_element_type=jnp.float32) + jnp.dot(
        final_samples, lower, preferred_element_type=jnp.float32
    )
    traces = traces.reshape(point_share, rows_dev, NT)
    time_index = jnp.arange(NT, dtype=jnp.int32)
    return jnp.where(time_index[None, None, :] < second_mute[:, :, None], traces, 0.0)


def solution(mesh):
    in_specs = (
        P(None, "freq", "rows", None),
        P("freq", "rows", None),
        P("freq", "rows", None),
        P("rows", None),
        P("freq", "rows"),
    )
    out_specs = P("freq", "rows", None)
    return jax.shard_map(
        on_device, mesh=mesh, in_specs=in_specs, out_specs=out_specs, check_vma=False
    )
```

profile of v0, /device:TPU:0, one launch (start us, length us, event | category | flops | bytes accessed | tf_op | source)
XLA Modules:
  0.0 245.4 jit_solution(14717921745920987155)
XLA Ops:
  6.5 0.7 all-gather.2.cloned.1.call-update
  7.3 1.0 copy.60
  8.3 6.3 %mul.70 = f32[2,288,36,128]{3,2,1,0:T(8,128)} broadcast(f32[2,288,36]{2,1,0:T(8,128)S(1)} %copy.60), dimensions={0,1,2} | broadcast | bytes 10699776 | tf_op jit(solution)/shard_map/mul | solution.py:33
  14.6 12.4 %mul.71 = f32[2,288,4608]{2,1,0:T(8,128)} reshape(f32[2,288,36,128]{3,2,1,0:T(8,128)} %mul.70) | data formatting | bytes 21233664 | tf_op jit(solution)/shard_map/mul | solution.py:33
  27.2 34.3 %all-gather.2.cloned.1.call-done = bf16[2,4608,128]{2,1,0:T(8,128)(2,1)} async-done(((bf16[2,288,128]{2,1,0:T(8,128)(2,1)}), bf16[2,4608,128]{2,1,0:T(8,128)(2,1)}) %all-gather.2.cloned.1.call-update) | async-done | bytes 2359312 | tf_op jit(solution)/shard_map/all_gather | solution.py:79
  61.5 9.3 %fusion.17 = f32[2,2,288,128]{3,2,0,1:T(8,128)S(1)} fusion(bf16[2,4608,128]{2,1,0:T(8,128)(2,1)} %all-gather.2.cloned.1.call-done, bf16[2,2,288,4608]{3,2,1,0:T(8,128)(2,1)} %param.5, f32[2,288,4608]{2,1,0:T(8,128)} %mul.71), kind=kOutput, calls=%fused_computation.22 | convolution fusion | flops 1374879744 | bytes 24182784 | tf_op jit(solution)/shard_map/kfsn,fnc->kfsc/dot_general | solution.py:76
  70.9 0.2 fusion.24
  71.2 0.9 copy.63
  72.1 4.4 %all-to-all-start = ((bf16[2,288,2,64]{1,2,0,3:T(2,128)(2,1)}), bf16[2,288,2,64]{1,2,0,3:T(2,128)(2,1)S(1)}, u32[]{:S(2)}, u32[]{:S(2)}) async-start(bf16[2,288,2,64]{1,2,0,3:T(2,128)(2,1)} %copy.63), calls=%async_computation | async-start | bytes 393216 | tf_op jit(solution)/shard_map/all_to_all | solution.py:85
  76.4 0.3 fusion.45
  76.8 6.6 %all-to-all-done = bf16[2,288,2,64]{1,2,0,3:T(2,128)(2,1)S(1)} async-done(((bf16[2,288,2,64]{1,2,0,3:T(2,128)(2,1)}), bf16[2,288,2,64]{1,2,0,3:T(2,128)(2,1)S(1)}, u32[]{:S(2)}, u32[]{:S(2)}) %all-to-all-start) | async-done | bytes 147488 | tf_op jit(solution)/shard_map/all_to_all | solution.py:85
  83.4 1.6 copy.66
  85.1 0.5 reshape.34
  85.6 1.4 fusion.32
  87.1 1.4 fusion.44
  88.5 6.4 %fusion.13 = bf16[32,2304]{1,0:T(8,128)(2,1)S(1)} fusion(f32[1024,2304]{1,0:T(8,128)S(1)} %fusion.44, f32[1024,2304]{1,0:T(8,128)S(1)} %fusion.32, s32[2304]{0:T(1024)S(1)} %lt.45, f32[16,1024]{1,0:T(8,128)S(1)} %get-tuple-element.14, f32[16,1024]{1,0:T(8,128)S(1)} %get-tuple-element.13), kind=kOutput, calls=%fused_computation.18 | convolution fusion | flops 913186816 | bytes 19162112 | tf_op jit(solution)/shard_map/dot_general | solution.py:64
  94.9 0.3 copy.67
  95.3 0.5 reshape.35
  95.7 2.3 copy.68
  98.0 3.6 %all-to-all-start.1 = ((bf16[16,288,2,8]{1,3,2,0:T(8,128)(2,1)}), bf16[16,288,2,8]{1,3,2,0:T(8,128)(2,1)S(1)}, u32[]{:S(2)}, u32[]{:S(2)}) async-start(bf16[16,288,2,8]{1,3,2,0:T(8,128)(2,1)} %copy.68), calls=%async_computation.1 | async-start | bytes 393216 | tf_op jit(solution)/shard_map/all_to_all | solution.py:98
  101.6 0.6 dynamic-slice
  102.8 5.2 %all-to-all-done.1 = bf16[16,288,2,8]{1,3,2,0:T(8,128)(2,1)S(1)} async-done(((bf16[16,288,2,8]{1,3,2,0:T(8,128)(2,1)}), bf16[16,288,2,8]{1,3,2,0:T(8,128)(2,1)S(1)}, u32[]{:S(2)}, u32[]{:S(2)}) %all-to-all-start.1) | async-done | bytes 147488 | tf_op jit(solution)/shard_map/all_to_all | solution.py:98
  108.0 8.6 %fusion.8 = f32[2,4608,2,128]{1,3,0,2:T(8,128)S(1)} fusion(bf16[2,288,128,1]{1,2,3,0:T(8,128)(2,1)S(1)} %bitcast.80, bf16[2,2,288,4608]{3,2,1,0:T(8,128)(2,1)} %param.5, f32[2,288,4608]{2,1,0:T(8,128)} %mul.71), kind=kOutput, calls=%fused_computation.11 | convolution fusion | flops 1374879744 | bytes 30818304 | tf_op jit(solution)/shard_map/kfsn,fsc->knfc/dot_general | solution.py:103
  116.6 0.6 slice_bitcast_fusion.1
  117.3 0.5 slice_add_fusion
  117.8 2.5 %pad_maximum_fusion = f32[4608,2,128]{0,2,1:T(8,128)} fusion(f32[4608,2,64]{0,2,1:T(8,128)S(1)} %get-tuple-element.6, f32[4608,2,64]{0,2,1:T(8,128)S(1)} %get-tuple-element.5), kind=kLoop, calls=%fused_computation.15 | loop fusion | flops 1179648 | bytes 9437184 | tf_op jit(solution)/shard_map/concatenate | solution.py:48
  120.3 8.0 %copy.73 = f32[4608,2,128]{2,1,0:T(2,128)} copy(f32[4608,2,128]{0,2,1:T(8,128)} %pad_maximum_fusion) | data formatting | bytes 9437184 | tf_op jit(solution)/shard_map/concatenate | solution.py:48
  128.4 93.2 %all-reduce.2 = bf16[4608,2,128]{2,1,0:T(2,128)(2,1)S(1)} all-reduce(f32[4608,2,128]{2,1,0:T(2,128)} %copy.73), channel_id=2, replica_groups=mesh['freq'=8,'rows'=16] {'rows'}, use_global_device_ids=true, to_apply=%region_0.1.clone | all-reduce | flops 1179648 | bytes 7077888
  222.1 9.2 %all_to_all.51 = bf16[288,2,2,64]{0,2,1,3:T(2,128)(2,1)S(1)} all-to-all(bf16[288,2,2,64]{0,2,1,3:T(2,128)(2,1)S(1)} %copy.75), channel_id=1, replica_groups=mesh['freq'=8,'rows'=16] {'freq'}, dimensions={3} | all-to-all | bytes 294912 | tf_op jit(solution)/shard_map/all_to_all | solution.py:108
  231.5 1.4 fusion.42
  233.0 1.4 convolution_add_fusion
  234.4 4.2 %fusion.3 = f32[8,288,1024]{2,1,0:T(8,128)} fusion(f32[8,288,1024]{2,1,0:T(8,128)S(1)} %bitcast.78, s32[8,288]{1,0:T(8,128)S(1)} %copy-done.2), kind=kLoop, calls=%fused_computation.6 | loop fusion | flops 4718592 | bytes 18883584 | tf_op jit(solution)/shard_map/jit(_where)/select_n | solution.py:116
  (25 shorter events, 1.2 us)
Async XLA Ops:
  6.5 20.4 %copy-start = (s32[288,64]{0,1:T(8,128)S(1)}, s32[288,64]{0,1:T(8,128)}, u32[]{:S(2)}) copy-start(s32[288,64]{0,1:T(8,128)} %param.8) | copy-start | bytes 221188
  6.5 55.0 %all-gather.2.cloned.1.call-start = ((), (), s32[]{:S(2)}) async-start(), calls=%async_computation.3 | async-start | bytes 2506752 | tf_op jit(solution)/shard_map/all_gather | solution.py:79
  72.1 11.3 %all-to-all-start = ((bf16[2,288,2,64]{1,2,0,3:T(2,128)(2,1)}), bf16[2,288,2,64]{1,2,0,3:T(2,128)(2,1)S(1)}, u32[]{:S(2)}, u32[]{:S(2)}) async-start(bf16[2,288,2,64]{1,2,0,3:T(2,128)(2,1)} %copy.63), calls=%async_computation | async-start | bytes 393216 | tf_op jit(solution)/shard_map/all_to_all | solution.py:85
  88.5 13.1 %copy-start.3 = (u32[128]{0:T(128)S(1)}, u32[128]{0:T(128)}, u32[]{:S(2)}) copy-start(u32[128]{0:T(128)} %constant.41) | copy-start | bytes 1540
  98.0 10.0 %all-to-all-start.1 = ((bf16[16,288,2,8]{1,3,2,0:T(8,128)(2,1)}), bf16[16,288,2,8]{1,3,2,0:T(8,128)(2,1)S(1)}, u32[]{:S(2)}, u32[]{:S(2)}) async-start(bf16[16,288,2,8]{1,3,2,0:T(8,128)(2,1)} %copy.68), calls=%async_computation.1 | async-start | bytes 393216 | tf_op jit(solution)/shard_map/all_to_all | solution.py:98
  232.9 1.4 copy-start.2
  234.4 4.2 %copy-start.1 = (s32[288,64]{0,1:T(8,128)S(1)}, s32[288,64]{0,1:T(8,128)}, u32[]{:S(2)}) copy-start(s32[288,64]{0,1:T(8,128)} %param.8) | copy-start | bytes 221188
Sparse Core Ops, SparseCore 0:
  9.8 51.6 all-gather.1
where the time goes:
time: 246 us; the launch traced here: 245 us
  blocking collectives  102 us (41%)
  waiting for transfers between devices  46.8 us (19%)
  local copies, waits for them, and re-layouts  36.1 us (15%)
  matrix products  30.1 us (12%)
  between operations  14.2 us (6%)
  starting transfers between devices  7.99 us (3%)
  other arithmetic  7.83 us (3%)
    unnamed x1, blocking collectives  93.2 us
    all_gather x1, waiting for transfers between devices, on_device(): lax.all_gather(focus, 'rows', axis=1, tiled=True)  34.3 us
    mul x2, local copies, waits for them, and re-layouts, decode(): reshaped * block_scale[None, :, :, :, None]  18.7 us
    dot_general x1, matrix products, on_device(): jnp.einsum('kfsn,fnc->kfsc', columns, lax.all_gather(focus, 'rows', axis=...  9.34 us
    all_to_all x1, blocking collectives, on_device(): lax.all_to_all(adjoint_half, 'freq', split_axis=3, concat_axis=1, tiled=T...  9.18 us
    dot_general x1, matrix products, on_device(): jnp.einsum('kfsn,fsc->knfc', columns, returned, preferred_element_type=jn...  8.6 us
    concatenate x1, local copies, waits for them, and re-layouts, combine_second(): jnp.concatenate([direct[..., :points] + crossed[..., points:], direct[......  8.04 us
    all_to_all x1, waiting for transfers between devices, on_device(): lax.all_to_all(focused.reshape(freq_dev, rows_dev, 2, points), 'freq', sp...  6.59 us
  transfers between devices with their start and end apart: 3, of which 3 were waited for; matrix products, arithmetic and copies ran while one was open for 9% of the time, Pallas kernels for 0%

commit v1 on v0

--- a/solution.py
+++ b/solution.py
@@ -76,7 +76,9 @@
     paired = jnp.einsum(
         "kfsn,fnc->kfsc",
         columns,
-        lax.all_gather(focus, "rows", axis=1, tiled=True),
+        jnp.concatenate(
+            lax.all_to_all(jnp.stack([focus] * lax.axis_size("rows")), "rows", 0, 0), axis=1
+        ),
         preferred_element_type=jnp.float32,
     )
     focused = combine_first(paired[0], paired[1], points).astype(jnp.bfloat16)

time: 246 us -> 220 us (0.89)
  waiting for transfers between devices: 46.8 us -> 23.5 us
  between operations: 14.2 us -> 0.92 us
  starting transfers between devices: 7.99 us -> 16.4 us
  local copies, waits for them, and re-layouts: 36.1 us -> 39.1 us
    all_gather x1 -> x0, waiting for transfers between devices: 34.3 us -> none  [on_device(): lax.all_gather(focus, 'rows', axis=1, tiled=True)]
    all_to_all x0 -> x1, waiting for transfers between devices: none -> 12 us  [on_device(): lax.all_to_all(jnp.stack([focus] * lax.axis_size('rows')), 'rows', 0, 0)]
    all_to_all x0 -> x1, starting transfers between devices: none -> 7.83 us  [on_device(): lax.all_to_all(jnp.stack([focus] * lax.axis_size('rows')), 'rows', 0, 0)]
    another operation x0 -> x1, local copies, waits for them, and re-layouts: none -> 2.8 us  [on_device(): jnp.stack([focus] * lax.axis_size('rows'))]
  transfers between devices with their start and end apart: 3 -> 3, of which waited for: 3 -> 3; matrix products, arithmetic and copies ran while one was open for 9% -> 10% of each run, Pallas kernels for 0% -> 0%
where the time goes in v1:
time: 220 us; the launch traced here: 219 us
  blocking collectives  102 us (46%)
  local copies, waits for them, and re-layouts  39.1 us (18%)
  matrix products  29.4 us (13%)
  waiting for transfers between devices  23.5 us (11%)
  starting transfers between devices  16.4 us (7%)
  other arithmetic  7.83 us (4%)
    unnamed x1, blocking collectives  92.7 us
    mul x2, local copies, waits for them, and re-layouts, decode(): reshaped * block_scale[None, :, :, :, None]  18.6 us
    all_to_all x1, waiting for transfers between devices, on_device(): lax.all_to_all(jnp.stack([focus] * lax.axis_size('rows')), 'rows', 0, 0)  12 us
    all_to_all x1, blocking collectives, on_device(): lax.all_to_all(adjoint_half, 'freq', split_axis=3, concat_axis=1, tiled=T...  9.44 us
    dot_general x1, matrix products, on_device(): jnp.einsum('kfsn,fnc->kfsc', columns, jnp.concatenate(lax.all_to_all(jnp....  8.74 us
    dot_general x1, matrix products, on_device(): jnp.einsum('kfsn,fsc->knfc', columns, returned, preferred_element_type=jn...  8.6 us
    concatenate x1, local copies, waits for them, and re-layouts, combine_second(): jnp.concatenate([direct[..., :points] + crossed[..., points:], direct[......  8.05 us
    all_to_all x1, starting transfers between devices, on_device(): lax.all_to_all(jnp.stack([focus] * lax.axis_size('rows')), 'rows', 0, 0)  7.83 us
  transfers between devices with their start and end apart: 3, of which 3 were waited for; matrix products, arithmetic and copies ran while one was open for 10% of the time, Pallas kernels for 0%

profile of v1, /device:TPU:0, one launch (start us, length us, event | category | flops | bytes accessed | tf_op | source)
XLA Modules:
  0.0 219.3 jit_solution(14663069467446629712)
XLA Ops:
  0.0 2.8 %stack.2 = bf16[16,2,288,128]{3,2,1,0:T(8,128)(2,1)} broadcast(bf16[2,288,128]{2,1,0:T(8,128)(2,1)} %param.7), dimensions={1,2,3} | broadcast | bytes 2506752 | tf_op jit(solution)/shard_map/stack | solution.py:80
  2.8 7.8 %all-to-all-start = ((bf16[16,2,288,128]{3,2,1,0:T(8,128)(2,1)}), bf16[16,2,288,128]{3,2,1,0:T(8,128)(2,1)S(1)}, u32[]{:S(2)}, u32[]{:S(2)}) async-start(bf16[16,2,288,128]{3,2,1,0:T(8,128)(2,1)} %stack.2), calls=%async_computation | async-start | bytes 4718592 | tf_op jit(solution)/shard_map/all_to_all | solution.py:80
  10.6 1.0 copy.61
  11.7 6.3 %mul.70 = f32[2,288,36,128]{3,2,1,0:T(8,128)} broadcast(f32[2,288,36]{2,1,0:T(8,128)S(1)} %copy.61), dimensions={0,1,2} | broadcast | bytes 10699776 | tf_op jit(solution)/shard_map/mul | solution.py:33
  18.0 12.4 %mul.71 = f32[2,288,4608]{2,1,0:T(8,128)} reshape(f32[2,288,36,128]{3,2,1,0:T(8,128)} %mul.70) | data formatting | bytes 21233664 | tf_op jit(solution)/shard_map/mul | solution.py:33
  30.6 12.0 %all-to-all-done = bf16[16,2,288,128]{3,2,1,0:T(8,128)(2,1)S(1)} async-done(((bf16[16,2,288,128]{3,2,1,0:T(8,128)(2,1)}), bf16[16,2,288,128]{3,2,1,0:T(8,128)(2,1)S(1)}, u32[]{:S(2)}, u32[]{:S(2)}) %all-to-all-start) | async-done | bytes 2359328 | tf_op jit(solution)/shard_map/all_to_all | solution.py:80
  42.8 8.7 %fusion.16 = f32[2,2,288,128]{3,2,0,1:T(8,128)S(1)} fusion(bf16[2,4608,128,1]{2,1,3,0:T(8,128)(2,1)S(1)} %bitcast.79, bf16[2,2,288,4608]{3,2,1,0:T(8,128)(2,1)} %param.5, f32[2,288,4608]{2,1,0:T(8,128)} %mul.71), kind=kOutput, calls=%fused_computation.21 | convolution fusion | flops 1374879744 | bytes 24182784 | tf_op jit(solution)/shard_map/kfsn,fnc->kfsc/dot_general | solution.py:76
  51.9 0.9 copy.65
  52.8 4.9 %all-to-all-start.1 = ((bf16[2,288,2,64]{1,2,0,3:T(2,128)(2,1)}), bf16[2,288,2,64]{1,2,0,3:T(2,128)(2,1)S(1)}, u32[]{:S(2)}, u32[]{:S(2)}) async-start(bf16[2,288,2,64]{1,2,0,3:T(2,128)(2,1)} %copy.65), calls=%async_computation.1 | async-start | bytes 393216 | tf_op jit(solution)/shard_map/all_to_all | solution.py:87
  57.7 0.3 fusion.42
  58.0 6.3 %all-to-all-done.1 = bf16[2,288,2,64]{1,2,0,3:T(2,128)(2,1)S(1)} async-done(((bf16[2,288,2,64]{1,2,0,3:T(2,128)(2,1)}), bf16[2,288,2,64]{1,2,0,3:T(2,128)(2,1)S(1)}, u32[]{:S(2)}, u32[]{:S(2)}) %all-to-all-start.1) | async-done | bytes 147488 | tf_op jit(solution)/shard_map/all_to_all | solution.py:87
  64.4 1.6 copy.68
  66.0 0.5 reshape.44
  66.6 1.4 fusion.29
  68.0 1.4 fusion.41
  69.5 6.4 %fusion.13 = bf16[32,2304]{1,0:T(8,128)(2,1)S(1)} fusion(f32[1024,2304]{1,0:T(8,128)S(1)} %fusion.41, f32[1024,2304]{1,0:T(8,128)S(1)} %fusion.29, s32[2304]{0:T(1024)S(1)} %lt.45, f32[16,1024]{1,0:T(8,128)S(1)} %get-tuple-element.14, f32[16,1024]{1,0:T(8,128)S(1)} %get-tuple-element.13), kind=kOutput, calls=%fused_computation.18 | convolution fusion | flops 913186816 | bytes 19162112 | tf_op jit(solution)/shard_map/dot_general | solution.py:64
  75.9 0.3 copy.69
  76.2 0.5 reshape.45
  76.7 2.3 %copy.70 = bf16[16,288,2,8]{1,3,2,0:T(8,128)(2,1)} copy(bf16[16,288,2,8]{0,2,3,1:T(2,128)(2,1)S(1)} %bitcast.81) | data formatting | bytes 294912 | tf_op jit(solution)/shard_map/transpose | solution.py:99
  79.0 3.6 %all-to-all-start.2 = ((bf16[16,288,2,8]{1,3,2,0:T(8,128)(2,1)}), bf16[16,288,2,8]{1,3,2,0:T(8,128)(2,1)S(1)}, u32[]{:S(2)}, u32[]{:S(2)}) async-start(bf16[16,288,2,8]{1,3,2,0:T(8,128)(2,1)} %copy.70), calls=%async_computation.2 | async-start | bytes 393216 | tf_op jit(solution)/shard_map/all_to_all | solution.py:100
  82.6 0.6 dynamic-slice
  83.9 5.1 %all-to-all-done.2 = bf16[16,288,2,8]{1,3,2,0:T(8,128)(2,1)S(1)} async-done(((bf16[16,288,2,8]{1,3,2,0:T(8,128)(2,1)}), bf16[16,288,2,8]{1,3,2,0:T(8,128)(2,1)S(1)}, u32[]{:S(2)}, u32[]{:S(2)}) %all-to-all-start.2) | async-done | bytes 147488 | tf_op jit(solution)/shard_map/all_to_all | solution.py:100
  89.0 8.6 %fusion.8 = f32[2,4608,2,128]{1,3,0,2:T(8,128)S(1)} fusion(bf16[2,288,128,1]{1,2,3,0:T(8,128)(2,1)S(1)} %bitcast.82, bf16[2,2,288,4608]{3,2,1,0:T(8,128)(2,1)} %param.5, f32[2,288,4608]{2,1,0:T(8,128)} %mul.71), kind=kOutput, calls=%fused_computation.11 | convolution fusion | flops 1374879744 | bytes 30818304 | tf_op jit(solution)/shard_map/kfsn,fsc->knfc/dot_general | solution.py:105
  97.6 0.6 slice_bitcast_fusion.1
  98.2 0.5 slice_add_fusion
  98.8 2.5 %pad_maximum_fusion = f32[4608,2,128]{0,2,1:T(8,128)} fusion(f32[4608,2,64]{0,2,1:T(8,128)S(1)} %get-tuple-element.6, f32[4608,2,64]{0,2,1:T(8,128)S(1)} %get-tuple-element.5), kind=kLoop, calls=%fused_computation.15 | loop fusion | flops 1179648 | bytes 9437184 | tf_op jit(solution)/shard_map/concatenate | solution.py:48
  101.3 8.1 %copy.75 = f32[4608,2,128]{2,1,0:T(2,128)} copy(f32[4608,2,128]{0,2,1:T(8,128)} %pad_maximum_fusion) | data formatting | bytes 9437184 | tf_op jit(solution)/shard_map/concatenate | solution.py:48
  109.3 92.7 %all-reduce.2 = bf16[4608,2,128]{2,1,0:T(2,128)(2,1)S(1)} all-reduce(f32[4608,2,128]{2,1,0:T(2,128)} %copy.75), channel_id=2, replica_groups=mesh['freq'=8,'rows'=16] {'rows'}, use_global_device_ids=true, to_apply=%region_0.1.clone | all-reduce | flops 1179648 | bytes 7077888
  202.5 9.4 %all_to_all.56 = bf16[288,2,2,64]{0,2,1,3:T(2,128)(2,1)S(1)} all-to-all(bf16[288,2,2,64]{0,2,1,3:T(2,128)(2,1)S(1)} %copy.77), channel_id=1, replica_groups=mesh['freq'=8,'rows'=16] {'freq'}, dimensions={3} | all-to-all | bytes 294912 | tf_op jit(solution)/shard_map/all_to_all | solution.py:110
  212.2 1.4 fusion.39
  213.7 1.4 convolution_add_fusion
  215.1 4.2 %fusion.3 = f32[8,288,1024]{2,1,0:T(8,128)} fusion(f32[8,288,1024]{2,1,0:T(8,128)S(1)} %bitcast.78, s32[8,288]{1,0:T(8,128)S(1)} %copy-done.2), kind=kLoop, calls=%fused_computation.6 | loop fusion | flops 4718592 | bytes 18883584 | tf_op jit(solution)/shard_map/jit(_where)/select_n | solution.py:118
  (26 shorter events, 1.5 us)
Async XLA Ops:
  0.0 30.3 %copy-start = (s32[288,64]{0,1:T(8,128)S(1)}, s32[288,64]{0,1:T(8,128)}, u32[]{:S(2)}) copy-start(s32[288,64]{0,1:T(8,128)} %param.8) | copy-start | bytes 221188
  2.8 39.8 %all-to-all-start = ((bf16[16,2,288,128]{3,2,1,0:T(8,128)(2,1)}), bf16[16,2,288,128]{3,2,1,0:T(8,128)(2,1)S(1)}, u32[]{:S(2)}, u32[]{:S(2)}) async-start(bf16[16,2,288,128]{3,2,1,0:T(8,128)(2,1)} %stack.2), calls=%async_computation | async-start | bytes 4718592 | tf_op jit(solution)/shard_map/all_to_all | solution.py:80
  52.8 11.6 %all-to-all-start.1 = ((bf16[2,288,2,64]{1,2,0,3:T(2,128)(2,1)}), bf16[2,288,2,64]{1,2,0,3:T(2,128)(2,1)S(1)}, u32[]{:S(2)}, u32[]{:S(2)}) async-start(bf16[2,288,2,64]{1,2,0,3:T(2,128)(2,1)} %copy.65), calls=%async_computation.1 | async-start | bytes 393216 | tf_op jit(solution)/shard_map/all_to_all | solution.py:87
  69.5 13.1 %copy-start.3 = (u32[128]{0:T(128)S(1)}, u32[128]{0:T(128)}, u32[]{:S(2)}) copy-start(u32[128]{0:T(128)} %constant.41) | copy-start | bytes 1540
  79.0 10.0 %all-to-all-start.2 = ((bf16[16,288,2,8]{1,3,2,0:T(8,128)(2,1)}), bf16[16,288,2,8]{1,3,2,0:T(8,128)(2,1)S(1)}, u32[]{:S(2)}, u32[]{:S(2)}) async-start(bf16[16,288,2,8]{1,3,2,0:T(8,128)(2,1)} %copy.70), calls=%async_computation.2 | async-start | bytes 393216 | tf_op jit(solution)/shard_map/all_to_all | solution.py:100
  213.7 1.4 copy-start.2
  215.1 4.2 %copy-start.1 = (s32[288,64]{0,1:T(8,128)S(1)}, s32[288,64]{0,1:T(8,128)}, u32[]{:S(2)}) copy-start(s32[288,64]{0,1:T(8,128)} %param.8) | copy-start | bytes 221188
